TPU v7x, 512 devices: a whole 4x8x8 slice. The times are simulated.
512 devices in a mesh: req: 64 (over x, y, core), head: 8 (over z).
Axes of the slice: x: 4, y: 8, z: 8, core: 2. Of those that a mesh axis runs over, the one named last changes fastest.
Arguments:
- hidden: bfloat16 [512, 4096], P(None, 'req'), may hold values from -16 to 16
- query_key_value_weight: bfloat16 [4096, 8, 768], P('req', 'head'), may hold values from -0.1875 to 0.1875
- output_weight: bfloat16 [4096, 4096], P('head', 'req'), may hold values from -0.375 to 0.375
- kv_pool: bfloat16 [4096, 8, 128, 256], P('req', 'head'), may hold values from -68 to 68
- lengths: int32 [512], P('req'), may hold values from 513 to 2048, as said below
- page_table: int32 [512, 16], P('req'), may hold values from 0 to 127, as said below
- send_slots: int32 [4096], P('req'), may hold values from 0 to 63, as said below
Outputs:
- attn_out: bfloat16 [512, 4096], P('head', 'req')
Inputs may be any that keep to these rules, and one draw needn't show every extreme that they name: `page_table`: A request's live positions name distinct slots of its group's store, and every other entry is 0. Slots below 64 are the group's own pool rows; slot 64 + s is the page that group s sends to it. Every group uses exactly 32 of the 64 pages sent to it, never for a long request. `send_slots`: every group sends one page to every group; rows whose page the receiver does not use name an arbitrary slot. In 16 of the groups one request is long (more than (15) * 128 tokens); all others hold at most 768 tokens. The new token sits at position lengths[r].
All inputs are finite; a program needn't handle non-finite values.
Results may differ from a plain program's by a relative error of at most 0.018.
Values may be sent and summed in bfloat16 or wider, within the bound.
A program may use at most 64 MiB of HBM per device.

v0:
```python
import jax
import jax.numpy as jnp
from jax import lax
from jax.sharding import PartitionSpec as P

ROPE_BASE = 500000.0
NEG_FILL = -1e30


def rotate(vectors, angles):
    half_width = vectors.shape[-1] // 2
    first_half = vectors[..., :half_width]
    second_half = vectors[..., half_width:]
    cosine = jnp.cos(angles)
    sine_part = jnp.sin(angles)
    return jnp.concatenate(
        [
            first_half * cosine - second_half * sine_part,
            second_half * cosine + first_half * sine_part,
        ],
        axis=-1,
    )


def rope_angles(lengths, width):
    exponent = jnp.arange(width // 2, dtype=jnp.float32) * (2.0 / width)
    inverse = 1.0 / ROPE_BASE**exponent
    return lengths.astype(jnp.float32)[:, None] * inverse[None, :]


def split_projection(projected_rows, lengths):
    angles = rope_angles(lengths, projected_rows.shape[-1])
    queries = rotate(projected_rows[:, :, :-2], angles[:, None, None, :]).astype(jnp.bfloat16)
    new_keys = rotate(projected_rows[:, :, -2], angles[:, None, :]).astype(jnp.bfloat16)
    new_values = projected_rows[:, :, -1].astype(jnp.bfloat16)
    return (queries, new_keys, new_values)


def page_stats(queries, pages, valid_tokens, score_scale):
    head_dim = pages.shape[-1] // 2
    scores = (
        jnp.einsum(
            "nhqd,nhtd->nhqt", queries, pages[..., :head_dim], preferred_element_type=jnp.float32
        )
        * score_scale
    )
    token_mask = jnp.arange(pages.shape[2])[None, None, None, :] < valid_tokens[:, None, None, None]
    masked = jnp.where(token_mask, scores, NEG_FILL)
    top_score = jnp.max(masked, axis=-1)
    weights = jnp.where(token_mask, jnp.exp(scores - top_score[..., None]), 0.0)
    weight_sum = jnp.sum(weights, axis=-1)
    weighted_values = jnp.einsum(
        "nhqt,nhtd->nhqd",
        weights.astype(jnp.bfloat16),
        pages[..., head_dim:],
        preferred_element_type=jnp.float32,
    )
    return (top_score, weight_sum, weighted_values)


def shards(hidden, query_key_value_weight, output_weight, kv_pool, lengths, page_table, send_slots):
    groups = lax.axis_size("req")
    local_count = lengths.shape[0]
    head_count = query_key_value_weight.shape[1]
    pool_slots = kv_pool.shape[0]
    page_len = kv_pool.shape[2]
    head_dim = kv_pool.shape[3] // 2
    per_head = query_key_value_weight.shape[2] // head_dim
    flat_weight = query_key_value_weight.reshape(
        query_key_value_weight.shape[0], head_count * per_head * head_dim
    )
    projected_rows = lax.psum_scatter(
        jnp.dot(hidden, flat_weight, preferred_element_type=jnp.float32),
        "req",
        scatter_dimension=0,
        tiled=True,
    )
    projected_rows = projected_rows.reshape(local_count, head_count, per_head, head_dim)
    queries, new_keys, new_values = split_projection(projected_rows, lengths)
    score_scale = head_dim ** (-0.5)
    self_scores = (
        jnp.sum(queries.astype(jnp.float32) * new_keys.astype(jnp.float32)[:, :, None, :], axis=-1)
        * score_scale
    )
    total_slots = pool_slots + groups
    places = jnp.arange(page_table.shape[1], dtype=jnp.int32)
    is_live = places[None, :] * page_len < lengths[:, None]
    tokens_in = jnp.clip(lengths[:, None] - places[None, :] * page_len, 0, page_len)
    table_hits = (
        page_table[:, :, None] == jnp.arange(total_slots, dtype=jnp.int32)[None, None, :]
    ) & is_live[:, :, None]
    owner_map = jnp.any(table_hits, axis=1).T
    valid_tokens = jnp.sum(jnp.where(table_hits, tokens_in[:, :, None], 0), axis=(0, 1))
    owner_index = jnp.sum(
        jnp.where(owner_map, jnp.arange(local_count, dtype=jnp.int32)[None, :], 0), axis=1
    )
    slot_queries = jnp.einsum(
        "nr,rhqd->nhqd", owner_map.astype(jnp.bfloat16), queries, preferred_element_type=jnp.float32
    ).astype(jnp.bfloat16)
    outgoing = kv_pool[send_slots]
    arrived = lax.all_to_all(outgoing, "req", split_axis=0, concat_axis=0, tiled=True)
    page_store = jnp.concatenate([kv_pool, arrived], axis=0)
    page_max, page_sum, page_acc = page_stats(slot_queries, page_store, valid_tokens, score_scale)
    owned_max = jnp.max(jnp.where(owner_map[:, :, None, None], page_max[:, None], NEG_FILL), axis=0)
    top_score = jnp.maximum(owned_max, self_scores)
    factors = jnp.exp(page_max - top_score[owner_index])
    owner_float = owner_map.astype(jnp.float32)
    self_weight = jnp.exp(self_scores - top_score)
    total_weight_sum = (
        jnp.einsum("nr,nhq->rhq", owner_float, factors * page_sum, precision=lax.Precision.HIGHEST)
        + self_weight
    )
    weighted_values = jnp.einsum(
        "nr,nhqd->rhqd", owner_float, factors[..., None] * page_acc, precision=lax.Precision.HIGHEST
    )
    weighted_values = (
        weighted_values + self_weight[..., None] * new_values.astype(jnp.float32)[:, :, None, :]
    )
    output_per_head = (
        (weighted_values / total_weight_sum[..., None])
        .astype(jnp.bfloat16)
        .reshape(local_count, head_count * (per_head - 2) * head_dim)
    )
    partial_out = jnp.dot(
        lax.all_gather(output_per_head, "req", axis=0, tiled=True),
        output_weight,
        preferred_element_type=jnp.float32,
    )
    return lax.psum_scatter(
        partial_out.astype(jnp.bfloat16), "head", scatter_dimension=0, tiled=True
    )


def solution(mesh):
    return jax.shard_map(
        shards,
        mesh=mesh,
        in_specs=(
            P(None, "req"),
            P("req", "head", None),
            P("head", "req"),
            P("req", "head", None, None),
            P("req"),
            P("req", None),
            P("req"),
        ),
        out_specs=P("head", "req"),
        check_vma=False,
    )
```

profile of v0, /device:TPU:2, one launch (start us, length us, event | category | flops | bytes accessed | tf_op | source)
XLA Modules:
  0.0 291.1 jit_solution(14235447509010207527)
XLA Ops:
  6.5 0.7 compare_select_fusion.1
  7.2 5.0 %gather_fusion = bf16[64,128,256]{2,1,0:T(8,128)(2,1)} fusion(bf16[64,128,256]{2,1,0:T(8,128)(2,1)} %bitcast.50, s32[1024]{0:T(1024)S(1)} %pad_clamp_fusion.1), kind=kCustom, calls=%fused_computation | custom fusion | bytes 8388864 | tf_op jit(solution)/shard_map/gather | solution.py:100
  12.2 11.1 %all-to-all-start = ((bf16[64,1,128,256]{3,2,1,0:T(8,128)(2,1)}), bf16[64,1,128,256]{3,2,1,0:T(8,128)(2,1)}, u32[]{:S(2)}, u32[]{:S(2)}) async-start(bf16[64,1,128,256]{3,2,1,0:T(8,128)(2,1)} %bitcast.53), calls=%async_computation.1 | async-start | bytes 8388608 | tf_op jit(solution)/shard_map/all_to_all | solution.py:101
  23.4 0.0 reduce-scatter.3.cloned.1.call-start
  23.4 1.6 fusion.25
  25.1 0.0 reduce-scatter.5.cloned.1.call-start
  25.2 0.1 broadcast_compare_fusion
  25.2 0.1 fusion.29
  25.4 0.1 subtract_clamp_fusion
  25.5 0.1 select_reduce_fusion.1
  25.6 0.1 multiply_cosine_fusion.1
  25.7 0.1 iota_compare_fusion
  25.8 155.3 %reduce-scatter.3.cloned.1.call-done = f32[8,768]{1,0:T(8,128)} async-done(((f32[512,768]{1,0:T(8,128)}), f32[8,768]{1,0:T(8,128)}) %reduce-scatter.3.cloned.1.call-update) | async-done | bytes 24592 | tf_op jit(solution)/shard_map/reduce_scatter | solution.py:72
  181.1 0.7 slice_bitcast_fusion
  181.8 0.1 fusion.46
  181.9 0.1 maximum_convert_fusion
  182.0 0.9 subtract_convert_fusion
  182.9 0.2 multiply_reduce_fusion
  183.0 0.7 fusion.44
  183.7 0.3 convolution_convert_fusion.1
  184.0 4.6 %select_reduce_fusion = (f32[128,4]{1,0:T(8,128)S(1)}, f32[128,4,128]{2,1,0:T(4,128)S(1)}) fusion(pred[128,128]{1,0:T(8,128)(4,1)S(1)} %iota_compare_fusion, bf16[64,1,128,256]{3,2,0,1:T(8,128)(2,1)} %bitcast.51, bf16[64,1,128,256]{3,2,0,1:T(8,128)(2,1)} %bitcast.8, bf16[128,4,128]{2,0,1:T(8,128)(2,1)S(1)} %convolution_convert_fusion.1), kind=kOutput, calls=%fused_computation.22 | convolution fusion | flops 19070464 | bytes 8800256 | tf_op jit(solution)/shard_map/nhqd,nhtd->nhqt/dot_general | solution.py:42
  188.6 0.1 copy.20
  188.6 0.1 select_reduce_fusion.2
  188.8 0.1 copy.21
  188.8 0.7 gather_fusion.1
  189.5 0.4 fusion.18
  189.9 3.5 %fusion.11 = f32[128,4,128]{2,1,0:T(4,128)S(1)} fusion(bf16[64,1,128,256]{3,2,0,1:T(8,128)(2,1)} %bitcast.8, bf16[64,1,128,256]{3,2,0,1:T(8,128)(2,1)} %bitcast.52, f32[128,4,128]{2,1,0:T(4,128)S(1)} %get-tuple-element.14, f32[128,4]{1,0:T(8,128)S(1)} %get-tuple-element.13, f32[128,4]{1,0:T(8,128)S(1)} %subtract_exponential_fusion, ...), kind=kOutput, calls=%fused_computation.12 | convolution fusion | flops 25427968 | bytes 8933376 | tf_op jit(solution)/shard_map/nhqt,nhtd->nhqd/dot_general | solution.py:52
  193.4 0.2 convolution_add_fusion.1
  193.6 0.2 fusion.16
  193.9 48.6 %all_gather.3 = bf16[512,512]{1,0:T(8,128)(2,1)S(1)} all-gather(bf16[8,512]{1,0:T(8,128)(2,1)S(1)} %fusion.16), channel_id=1, replica_groups=mesh['req'=64,'head'=8] {'req'}, dimensions={0}, use_global_device_ids=true | all-gather | bytes 532480 | tf_op jit(solution)/shard_map/all_gather | solution.py:125
  242.5 0.9 convolution_convert_fusion
  243.4 40.8 %reduce-scatter.5.cloned.1.call-done = bf16[64,64]{1,0:T(8,128)(2,1)} async-done(((bf16[512,64]{1,0:T(8,128)(2,1)}), bf16[64,64]{1,0:T(8,128)(2,1)}) %reduce-scatter.5.cloned.1.call-update) | async-done | bytes 8208 | tf_op jit(solution)/shard_map/reduce_scatter | solution.py:129
  (22 shorter events, 0.2 us)
Async XLA Ops:
  6.5 16.9 %copy-start = (bf16[64,1,768]{2,0,1:T(8,128)(2,1)S(1)}, bf16[64,1,768]{2,0,1:T(8,128)(2,1)}, u32[]{:S(2)}) copy-start(bf16[64,1,768]{2,0,1:T(8,128)(2,1)} %param.8) | copy-start | bytes 294916
  12.2 11.2 %copy-start.2 = (bf16[512,64]{0,1:T(8,128)(2,1)S(1)}, bf16[512,64]{0,1:T(8,128)(2,1)}, u32[]{:S(2)}) copy-start(bf16[512,64]{0,1:T(8,128)(2,1)} %param.7) | copy-start | bytes 196612
  12.2 12.9 %copy-start.4 = (s32[8]{0:T(128)S(1)}, s32[8]{0:T(128)}, u32[]{:S(2)}) copy-start(s32[8]{0:T(128)} %param.11) | copy-start | bytes 100
  12.2 13.0 %copy-start.3 = (s32[8,16]{1,0:T(8,128)S(1)}, s32[8,16]{1,0:T(8,128)}, u32[]{:S(2)}) copy-start(s32[8,16]{1,0:T(8,128)} %param.12) | copy-start | bytes 1540
  12.2 171.8 %all-to-all-start = ((bf16[64,1,128,256]{3,2,1,0:T(8,128)(2,1)}), bf16[64,1,128,256]{3,2,1,0:T(8,128)(2,1)}, u32[]{:S(2)}, u32[]{:S(2)}) async-start(bf16[64,1,128,256]{3,2,1,0:T(8,128)(2,1)} %bitcast.53), calls=%async_computation.1 | async-start | bytes 8388608 | tf_op jit(solution)/shard_map/all_to_all | solution.py:101
  23.4 157.7 %reduce-scatter.3.cloned.1.call-start = ((), (), s32[]{:S(2)}) async-start(), calls=%async_computation.3 | async-start | bytes 1597440 | tf_op jit(solution)/shard_map/reduce_scatter | solution.py:72
  25.1 259.2 %reduce-scatter.5.cloned.1.call-start = ((), (), s32[]{:S(2)}) async-start(), calls=%async_computation.4 | async-start | bytes 147456 | tf_op jit(solution)/shard_map/reduce_scatter | solution.py:129
  189.9 52.6 %copy-start.1 = (bf16[512,64]{0,1:T(8,128)(2,1)S(1)}, bf16[512,64]{0,1:T(8,128)(2,1)}, u32[]{:S(2)}) copy-start(bf16[512,64]{0,1:T(8,128)(2,1)} %param.9) | copy-start | bytes 196612
Sparse Core Ops, SparseCore 0:
  28.8 152.2 reduce-scatter.2
  243.6 40.6 reduce-scatter.4
where the time goes:
time: 292 us; the launch traced here: 291 us
  waiting for transfers between devices  196 us (67%)
  blocking collectives  48.6 us (17%)
  between operations  13.5 us (5%)
  matrix products  11.3 us (4%)
  starting transfers between devices  11.2 us (4%)
  local copies, waits for them, and re-layouts  6.47 us (2%)
  other arithmetic  3.76 us (1%)
    reduce_scatter x1, waiting for transfers between devices, shards(): lax.psum_scatter(jnp.dot(hidden, flat_weight, preferred_element_type=jnp....  155 us
    all_gather x1, blocking collectives, shards(): lax.all_gather(output_per_head, 'req', axis=0, tiled=True)  48.6 us
    reduce_scatter x1, waiting for transfers between devices, shards(): lax.psum_scatter(partial_out.astype(jnp.bfloat16), 'head', scatter_dimens...  40.8 us
    all_to_all x1, starting transfers between devices, shards(): lax.all_to_all(outgoing, 'req', split_axis=0, concat_axis=0, tiled=True)  11.1 us
  transfers between devices with their start and end apart: 3, of which 2 were waited for; matrix products, arithmetic and copies ran while one was open for 2% of the time, Pallas kernels for 0%

commit v1 on v0

--- a/solution.py
+++ b/solution.py
@@ -122,7 +122,9 @@
         .reshape(local_count, head_count * (per_head - 2) * head_dim)
     )
     partial_out = jnp.dot(
-        lax.all_gather(output_per_head, "req", axis=0, tiled=True),
+        jnp.concatenate(
+            lax.all_to_all(jnp.stack([output_per_head] * lax.axis_size("req")), "req", 0, 0), axis=0
+        ),
         output_weight,
         preferred_element_type=jnp.float32,
     )

time: 292 us -> 266 us (0.911)
  blocking collectives: 48.6 us -> 25.1 us
    all_gather x1 -> x0, blocking collectives: 48.6 us -> none  [shards(): lax.all_gather(output_per_head, 'req', axis=0, tiled=True)]
    all_to_all x0 -> x1, blocking collectives: none -> 25.1 us  [shards(): lax.all_to_all(jnp.stack([output_per_head] * lax.axis_size('req')), 'req'...]
where the time goes in v1:
time: 266 us; the launch traced here: 265 us
  waiting for transfers between devices  194 us (73%)
  blocking collectives  25.1 us (9%)
  between operations  13.5 us (5%)
  matrix products  11.3 us (4%)
  starting transfers between devices  11.2 us (4%)
  local copies, waits for them, and re-layouts  6.51 us (2%)
  other arithmetic  3.76 us (1%)
    reduce_scatter x1, waiting for transfers between devices, shards(): lax.psum_scatter(jnp.dot(hidden, flat_weight, preferred_element_type=jnp....  155 us
    reduce_scatter x1, waiting for transfers between devices, shards(): lax.psum_scatter(partial_out.astype(jnp.bfloat16), 'head', scatter_dimens...  38.5 us
    all_to_all x1, blocking collectives, shards(): lax.all_to_all(jnp.stack([output_per_head] * lax.axis_size('req')), 'req'...  25.1 us
    all_to_all x1, starting transfers between devices, shards(): lax.all_to_all(outgoing, 'req', split_axis=0, concat_axis=0, tiled=True)  11.1 us
  transfers between devices with their start and end apart: 3, of which 2 were waited for; matrix products, arithmetic and copies ran while one was open for 2% of the time, Pallas kernels for 0%

profile of v1, /device:TPU:2, one launch (start us, length us, event | category | flops | bytes accessed | tf_op | source)
XLA Modules:
  0.0 265.3 jit_solution(14369854928838752136)
XLA Ops:
  6.5 0.7 compare_select_fusion.1
  7.2 5.0 %gather_fusion = bf16[64,128,256]{2,1,0:T(8,128)(2,1)} fusion(bf16[64,128,256]{2,1,0:T(8,128)(2,1)} %bitcast.52, s32[1024]{0:T(1024)S(1)} %pad_clamp_fusion.1), kind=kCustom, calls=%fused_computation | custom fusion | bytes 8388864 | tf_op jit(solution)/shard_map/gather | solution.py:100
  12.2 11.1 %all-to-all-start = ((bf16[64,1,128,256]{3,2,1,0:T(8,128)(2,1)}), bf16[64,1,128,256]{3,2,1,0:T(8,128)(2,1)}, u32[]{:S(2)}, u32[]{:S(2)}) async-start(bf16[64,1,128,256]{3,2,1,0:T(8,128)(2,1)} %bitcast.55), calls=%async_computation.1 | async-start | bytes 8388608 | tf_op jit(solution)/shard_map/all_to_all | solution.py:101
  23.4 0.0 reduce-scatter.3.cloned.1.call-start
  23.4 1.6 fusion.26
  25.1 0.0 reduce-scatter.5.cloned.1.call-start
  25.2 0.1 broadcast_compare_fusion
  25.2 0.1 fusion.30
  25.4 0.1 subtract_clamp_fusion
  25.5 0.1 select_reduce_fusion.1
  25.6 0.1 multiply_cosine_fusion.1
  25.7 0.1 iota_compare_fusion
  25.8 155.3 %reduce-scatter.3.cloned.1.call-done = f32[8,768]{1,0:T(8,128)} async-done(((f32[512,768]{1,0:T(8,128)}), f32[8,768]{1,0:T(8,128)}) %reduce-scatter.3.cloned.1.call-update) | async-done | bytes 24592 | tf_op jit(solution)/shard_map/reduce_scatter | solution.py:72
  181.1 0.7 slice_bitcast_fusion
  181.8 0.1 fusion.47
  181.9 0.1 maximum_convert_fusion
  182.0 0.9 subtract_convert_fusion
  182.9 0.2 multiply_reduce_fusion
  183.0 0.7 fusion.45
  183.7 0.3 convolution_convert_fusion.1
  184.0 4.6 %select_reduce_fusion = (f32[128,4]{1,0:T(8,128)S(1)}, f32[128,4,128]{2,1,0:T(4,128)S(1)}) fusion(pred[128,128]{1,0:T(8,128)(4,1)S(1)} %iota_compare_fusion, bf16[64,1,128,256]{3,2,0,1:T(8,128)(2,1)} %bitcast.53, bf16[64,1,128,256]{3,2,0,1:T(8,128)(2,1)} %bitcast.8, bf16[128,4,128]{2,0,1:T(8,128)(2,1)S(1)} %convolution_convert_fusion.1), kind=kOutput, calls=%fused_computation.23 | convolution fusion | flops 19070464 | bytes 8800256 | tf_op jit(solution)/shard_map/nhqd,nhtd->nhqt/dot_general | solution.py:42
  188.6 0.1 copy.20
  188.6 0.1 select_reduce_fusion.2
  188.8 0.1 copy.21
  188.8 0.7 gather_fusion.1
  189.5 0.4 fusion.19
  189.9 3.5 %fusion.11 = f32[128,4,128]{2,1,0:T(4,128)S(1)} fusion(bf16[64,1,128,256]{3,2,0,1:T(8,128)(2,1)} %bitcast.8, bf16[64,1,128,256]{3,2,0,1:T(8,128)(2,1)} %bitcast.54, f32[128,4,128]{2,1,0:T(4,128)S(1)} %get-tuple-element.14, f32[128,4]{1,0:T(8,128)S(1)} %get-tuple-element.13, f32[128,4]{1,0:T(8,128)S(1)} %subtract_exponential_fusion, ...), kind=kOutput, calls=%fused_computation.12 | convolution fusion | flops 25427968 | bytes 8933376 | tf_op jit(solution)/shard_map/nhqt,nhtd->nhqd/dot_general | solution.py:52
  193.4 0.2 convolution_add_fusion.1
  193.6 0.2 fusion.16
  193.9 25.1 %all_to_all.10 = bf16[64,8,512]{2,1,0:T(8,128)(2,1)S(1)} all-to-all(bf16[64,8,512]{2,1,0:T(8,128)(2,1)S(1)} %stack.3), channel_id=1, replica_groups=mesh['req'=64,'head'=8] {'req'}, dimensions={0} | all-to-all | bytes 1048576 | tf_op jit(solution)/shard_map/all_to_all | solution.py:126
  219.0 0.9 convolution_convert_fusion
  219.9 38.5 %reduce-scatter.5.cloned.1.call-done = bf16[64,64]{1,0:T(8,128)(2,1)} async-done(((bf16[512,64]{1,0:T(8,128)(2,1)}), bf16[64,64]{1,0:T(8,128)(2,1)}) %reduce-scatter.5.cloned.1.call-update) | async-done | bytes 8208 | tf_op jit(solution)/shard_map/reduce_scatter | solution.py:131
  (23 shorter events, 0.2 us)
Async XLA Ops:
  6.5 16.9 %copy-start = (bf16[64,1,768]{2,0,1:T(8,128)(2,1)S(1)}, bf16[64,1,768]{2,0,1:T(8,128)(2,1)}, u32[]{:S(2)}) copy-start(bf16[64,1,768]{2,0,1:T(8,128)(2,1)} %param.8) | copy-start | bytes 294916
  12.2 11.2 %copy-start.2 = (bf16[512,64]{0,1:T(8,128)(2,1)S(1)}, bf16[512,64]{0,1:T(8,128)(2,1)}, u32[]{:S(2)}) copy-start(bf16[512,64]{0,1:T(8,128)(2,1)} %param.7) | copy-start | bytes 196612
  12.2 12.9 %copy-start.4 = (s32[8]{0:T(128)S(1)}, s32[8]{0:T(128)}, u32[]{:S(2)}) copy-start(s32[8]{0:T(128)} %param.11) | copy-start | bytes 100
  12.2 13.0 %copy-start.3 = (s32[8,16]{1,0:T(8,128)S(1)}, s32[8,16]{1,0:T(8,128)}, u32[]{:S(2)}) copy-start(s32[8,16]{1,0:T(8,128)} %param.12) | copy-start | bytes 1540
  12.2 171.8 %all-to-all-start = ((bf16[64,1,128,256]{3,2,1,0:T(8,128)(2,1)}), bf16[64,1,128,256]{3,2,1,0:T(8,128)(2,1)}, u32[]{:S(2)}, u32[]{:S(2)}) async-start(bf16[64,1,128,256]{3,2,1,0:T(8,128)(2,1)} %bitcast.55), calls=%async_computation.1 | async-start | bytes 8388608 | tf_op jit(solution)/shard_map/all_to_all | solution.py:101
  23.4 157.7 %reduce-scatter.3.cloned.1.call-start = ((), (), s32[]{:S(2)}) async-start(), calls=%async_computation.4 | async-start | bytes 1597440 | tf_op jit(solution)/shard_map/reduce_scatter | solution.py:72
  25.1 233.4 %reduce-scatter.5.cloned.1.call-start = ((), (), s32[]{:S(2)}) async-start(), calls=%async_computation.5 | async-start | bytes 147456 | tf_op jit(solution)/shard_map/reduce_scatter | solution.py:131
  189.9 29.1 %copy-start.1 = (bf16[512,64]{0,1:T(8,128)(2,1)S(1)}, bf16[512,64]{0,1:T(8,128)(2,1)}, u32[]{:S(2)}) copy-start(bf16[512,64]{0,1:T(8,128)(2,1)} %param.9) | copy-start | bytes 196612
Sparse Core Ops, SparseCore 0:
  28.8 152.2 reduce-scatter.2
  220.1 38.3 reduce-scatter.4
